TPU v7x, 128 devices: a whole 4x4x4 slice. The times are simulated.
128 devices in a mesh: row: 8 (over y, core), col: 16 (over z, x).
Axes of the slice: x: 4, y: 4, z: 4, core: 2. Of those that a mesh axis runs over, the one named last changes fastest.
Arguments:
- wavefunction: bfloat16 [32, 16, 256, 256], P('row', 'col'), may hold values from -6 to 6
- env_left: bfloat16 [16, 32, 2, 256, 256], P('col', 'row'), may hold values from -0.25 to 0.25
- left_src: int32 [16, 32, 2], P('col', 'row'), may hold values from 0 to 3
- two_site: bfloat16 [16, 16, 16], P('col'), may hold values from -1.5 to 1.5
- env_right: bfloat16 [16, 32, 256, 256], P('col', 'row'), may hold values from -0.09375 to 0.09375
- right_loc: int32 [32, 16], P('row', 'col'), may hold values from 0 to 3
- left_size: int32 [32], P('row'), may hold values from 128 to 256
- right_size: int32 [32], P('row'), may hold values from 128 to 256
Outputs:
- applied: bfloat16 [32, 16, 256, 256], P('row', 'col')
All inputs are finite; a program needn't handle non-finite values.
Results may differ from a plain program's by a relative error of at most 0.018.
Values may be sent and summed in bfloat16 or wider, within the bound.
No kernel may reach another device: no remote copies, remote signals or barrier semaphores. Data moves between devices by JAX's collectives and lax.ppermute only.
A program may use at most 128 MiB of HBM per device.

v0:
```python
import jax
import jax.numpy as jnp
from jax import lax
from jax.sharding import PartitionSpec as P


def per_device(
    wavefunction, env_left, left_src, two_site, env_right, right_loc, left_size, right_size
):
    whole, whole_loc = (
        lax.all_gather(wavefunction, "col", axis=1, tiled=True),
        lax.all_gather(right_loc, "col", axis=1, tiled=True),
    )
    local_tiles = wavefunction.shape[0]
    tile_width = wavefunction.shape[3]
    mixed_rows = []
    for position in range(local_tiles):
        blocks = whole[left_src[0, position]]
        left_part = jnp.einsum(
            "kxy,ksyz->sxz", env_left[0, position], blocks, preferred_element_type=jnp.float32
        ).astype(jnp.bfloat16)
        mixed_rows.append(
            jnp.einsum(
                "ts,sxz->txz", two_site[0], left_part, preferred_element_type=jnp.float32
            ).astype(jnp.bfloat16)
        )
    mixed = jnp.stack(mixed_rows)
    col_iota = lax.broadcasted_iota(jnp.int32, (1, 1, tile_width), 2)
    received, recv_loc = (
        lax.all_to_all(mixed, "row", split_axis=1, concat_axis=0, tiled=True),
        lax.all_to_all(whole_loc, "row", split_axis=1, concat_axis=0, tiled=True),
    )
    pieces = []
    for column in range(received.shape[1]):
        chosen = env_right[0][recv_loc[:, column]]
        product = jnp.einsum(
            "axy,azy->axz", received[:, column], chosen, preferred_element_type=jnp.float32
        )
        col_limit = right_size[recv_loc[:, column]]
        inside = col_iota < col_limit[:, None, None]
        pieces.append(jnp.where(inside, product, 0.0).astype(jnp.bfloat16))
    term = lax.all_to_all(jnp.stack(pieces, axis=1), "row", split_axis=0, concat_axis=1, tiled=True)
    summed = lax.psum_scatter(
        term.astype(jnp.float32).astype(jnp.bfloat16), "col", scatter_dimension=1, tiled=True
    ).astype(jnp.float32)
    row_iota = lax.broadcasted_iota(jnp.int32, summed.shape, 2)
    inside_rows = row_iota < left_size[:, None, None, None]
    return jnp.where(inside_rows, summed, 0.0).astype(jnp.bfloat16)


def solution(mesh):
    placed = (
        P("row", "col", None, None),
        P("col", "row", None, None, None),
        P("col", "row", None),
        P("col", None, None),
        P("col", "row", None, None),
        P("row", "col"),
        P("row"),
        P("row"),
    )
    return jax.shard_map(
        per_device,
        mesh=mesh,
        in_specs=placed,
        out_specs=P("row", "col", None, None),
        check_vma=False,
    )
```

profile of v0, /device:TPU:1, one launch (start us, length us, event | category | flops | bytes accessed | tf_op | source)
XLA Modules:
  0.0 596.2 jit_solution(1501007717909477833)
XLA Ops:
  7.3 18.3 %all-gather = s32[16,1,4]{2,1,0:T(1,128)S(1)} all-gather(s32[1,1,4]{2,1,0:T(1,128)} %bitcast.158), channel_id=1, replica_groups=mesh['row'=8,'col'=16] {'col'}, dimensions={0}, use_global_device_ids=true | all-gather | bytes 272 | tf_op jit(solution)/shard_map/all_gather | solution.py:12
  26.3 9.6 %all-to-all-start = ((s32[4,8,2]{0,2,1:T(2,128)}), s32[4,8,2]{0,2,1:T(2,128)S(1)}, u32[]{:S(2)}, u32[]{:S(2)}) async-start(s32[4,8,2]{0,2,1:T(2,128)} %bitcast.3), calls=%async_computation | async-start | bytes 16384 | tf_op jit(solution)/shard_map/all_to_all | solution.py:31
  37.0 46.7 %all-gather.3.cloned.1.call-done = bf16[4,16,256,256]{3,2,1,0:T(8,128)(2,1)} async-done(((bf16[4,1,256,256]{3,2,1,0:T(8,128)(2,1)}), bf16[4,16,256,256]{3,2,1,0:T(8,128)(2,1)}) %all-gather.3.cloned.1.call-update) | async-done | bytes 8388624 | tf_op jit(solution)/shard_map/all_gather | solution.py:11
  83.7 6.0 fusion.62
  92.5 4.2 gather_fusion.7
  105.1 4.2 gather_fusion.2
  109.3 4.2 gather_fusion.3
  113.6 4.2 gather_fusion.8
  128.5 4.2 fusion.34
  144.0 4.9 fusion.31
  148.8 4.6 copy.38
  163.8 4.9 fusion.28
  180.6 4.9 fusion.37
  191.0 5.7 pad_maximum_fusion
  196.7 9.6 %copy.45 = bf16[4,16,256,256]{3,2,0,1:T(8,128)(2,1)} copy(bf16[4,16,256,256]{3,1,2,0:T(8,128)(2,1)} %pad_maximum_fusion) | data formatting | bytes 16777216 | tf_op jit(solution)/shard_map/stack | solution.py:27
  206.3 5.6 all-to-all-start.1
  220.9 85.0 %all-to-all-done.1 = bf16[4,16,256,256]{3,2,0,1:T(8,128)(2,1)} async-done(((bf16[4,16,256,256]{3,2,0,1:T(8,128)(2,1)}), bf16[4,16,256,256]{3,2,0,1:T(8,128)(2,1)}, u32[]{:S(2)}, u32[]{:S(2)}) %all-to-all-start.1) | async-done | bytes 8388640 | tf_op jit(solution)/shard_map/all_to_all | solution.py:30
  305.9 7.8 %copy.46 = bf16[4,8,2,256,256]{4,3,0,1,2:T(8,128)(2,1)} copy(bf16[4,8,2,256,256]{4,3,0,2,1:T(8,128)(2,1)} %bitcast.44) | data formatting | bytes 16777216 | tf_op jit(solution)/shard_map/all_to_all | solution.py:30
  313.6 5.8 fusion
  324.2 6.2 %pad_maximum_fusion.1 = bf16[32,2,256,256]{3,2,0,1:T(8,128)(2,1)} fusion(bf16[32,1,256,256]{3,2,0,1:T(8,128)(2,1)} %fusion.1, bf16[32,1,256,256]{3,2,0,1:T(8,128)(2,1)S(1)} %copy-done.9), kind=kLoop, calls=%fused_computation.11 | loop fusion | flops 4194304 | bytes 16777216 | tf_op jit(solution)/shard_map/stack | solution.py:42
  330.4 7.6 %copy.47 = bf16[32,2,256,256]{3,2,1,0:T(8,128)(2,1)} copy(bf16[32,2,256,256]{3,2,0,1:T(8,128)(2,1)} %pad_maximum_fusion.1) | data formatting | bytes 16777216 | tf_op jit(solution)/shard_map/stack | solution.py:42
  338.0 101.5 %all_to_all.55 = bf16[32,2,256,256]{3,2,1,0:T(8,128)(2,1)} all-to-all(bf16[32,2,256,256]{3,2,1,0:T(8,128)(2,1)} %copy.47), channel_id=1, replica_groups=mesh['row'=8,'col'=16] {'row'}, dimensions={0} | all-to-all | bytes 16777216 | tf_op jit(solution)/shard_map/all_to_all | solution.py:42
  439.5 7.6 %copy.48 = bf16[4,8,2,256,256]{4,3,2,1,0:T(8,128)(2,1)} copy(bf16[4,8,2,256,256]{4,3,2,0,1:T(8,128)(2,1)} %bitcast.153) | data formatting | bytes 16777216 | tf_op jit(solution)/shard_map/all_to_all | solution.py:42
  448.4 138.3 %all-reduce.3.cloned.1.call-done = bf16[4,16,256,256]{3,2,1,0:T(8,128)(2,1)} async-done(((bf16[4,16,256,256]{3,2,1,0:T(8,128)(2,1)}), bf16[4,16,256,256]{3,2,1,0:T(8,128)(2,1)}) %all-reduce.3.cloned.1.call-update) | async-done | bytes 8388624
  (75 shorter events, 81.2 us)
Async XLA Ops:
  6.5 206.2 %copy-start = (bf16[1,4,256,256]{3,2,1,0:T(8,128)(2,1)S(1)}, bf16[1,4,256,256]{3,2,1,0:T(8,128)(2,1)}, u32[]{:S(2)}) copy-start(bf16[1,4,256,256]{3,2,1,0:T(8,128)(2,1)} %param.12) | copy-start | bytes 1572868
  6.5 77.1 %all-gather.3.cloned.1.call-start = ((), (), s32[]{:S(2)}) async-start(), calls=%async_computation.3 | async-start | bytes 8912896 | tf_op jit(solution)/shard_map/all_gather | solution.py:11
  26.3 180.1 %all-to-all-start = ((s32[4,8,2]{0,2,1:T(2,128)}), s32[4,8,2]{0,2,1:T(2,128)S(1)}, u32[]{:S(2)}, u32[]{:S(2)}) async-start(s32[4,8,2]{0,2,1:T(2,128)} %bitcast.3), calls=%async_computation | async-start | bytes 16384 | tf_op jit(solution)/shard_map/all_to_all | solution.py:31
  124.4 4.1 copy-start.10
  148.8 4.6 copy-start.11
  153.4 2.1 copy-start.1
  155.5 6.0 copy-start.4
  174.1 4.1 copy-start.3
  188.8 1.6 copy-start.5
  188.8 2.2 copy-start.6
  206.3 5.6 copy-start.12
  206.3 99.5 %all-to-all-start.1 = ((bf16[4,16,256,256]{3,2,0,1:T(8,128)(2,1)}), bf16[4,16,256,256]{3,2,0,1:T(8,128)(2,1)}, u32[]{:S(2)}, u32[]{:S(2)}) async-start(bf16[4,16,256,256]{3,2,0,1:T(8,128)(2,1)} %copy.45), calls=%async_computation.1 | async-start | bytes 16777216 | tf_op jit(solution)/shard_map/all_to_all | solution.py:30
  212.0 374.7 %all-reduce.3.cloned.1.call-start = ((), (), s32[]{:S(2)}) async-start(), calls=%async_computation.4 | async-start | bytes 16777216
  305.8 7.8 %copy-start.8 = (bf16[32,256,256]{2,1,0:T(8,128)(2,1)S(1)}, bf16[32,256,256]{2,1,0:T(8,128)(2,1)}, u32[]{:S(2)}) copy-start(bf16[32,256,256]{2,1,0:T(8,128)(2,1)} %gather_fusion) | copy-start | bytes 12582916
  313.6 5.8 copy-start.2
  313.6 7.3 %copy-start.7 = (bf16[32,256,256]{2,1,0:T(8,128)(2,1)S(1)}, bf16[32,256,256]{2,1,0:T(8,128)(2,1)}, u32[]{:S(2)}) copy-start(bf16[32,256,256]{2,1,0:T(8,128)(2,1)} %gather_fusion.1) | copy-start | bytes 12582916
  321.0 3.3 copy-start.9
  447.1 0.7 copy-start.14
  447.1 139.6 %copy-start.13 = (s32[4]{0:T(128)S(1)}, s32[4]{0:T(128)}, u32[]{:S(2)}) copy-start(s32[4]{0:T(128)} %param.14) | copy-start | bytes 52
Sparse Core Ops, SparseCore 0:
  9.5 74.1 all-gather.2
  447.3 139.3 all-reduce.2
where the time goes:
time: 598 us; the launch traced here: 596 us
  waiting for transfers between devices  271 us (45%)
  local copies, waits for them, and re-layouts  125 us (21%)
  blocking collectives  120 us (20%)
  matrix products  34.7 us (6%)
  other arithmetic  17.2 us (3%)
  starting transfers between devices  15.2 us (3%)
  between operations  13.6 us (2%)
    unnamed x3, waiting for transfers between devices  139 us
    all_to_all x1, blocking collectives, per_device(): lax.all_to_all(jnp.stack(pieces, axis=1), 'row', split_axis=0, concat_axi...  101 us
    all_to_all x1, waiting for transfers between devices, per_device(): lax.all_to_all(mixed, 'row', split_axis=1, concat_axis=0, tiled=True)  85 us
    gather x17, local copies, waits for them, and re-layouts, per_device(): blocks = whole[left_src[0, position]]  65.5 us
    all_gather x1, waiting for transfers between devices, per_device(): lax.all_gather(wavefunction, 'col', axis=1, tiled=True)  46.7 us
    dot_general x4, matrix products, per_device(): jnp.einsum('kxy,ksyz->sxz', env_left[0, position], blocks, preferred_elem...  18.8 us
    all_gather x1, blocking collectives, per_device(): lax.all_gather(right_loc, 'col', axis=1, tiled=True)  18.3 us
    convert_element_type x4, local copies, waits for them, and re-layouts, per_device(): left_part = jnp.einsum('kxy,ksyz->sxz', env_left[0, position], blocks, pr...  14.6 us
  transfers between devices with their start and end apart: 4, of which 3 were waited for; matrix products, arithmetic and copies ran while one was open for 22% of the time, Pallas kernels for 0%

commit v1 on v0

--- a/solution.py
+++ b/solution.py
@@ -7,8 +7,11 @@
 def per_device(
     wavefunction, env_left, left_src, two_site, env_right, right_loc, left_size, right_size
 ):
+    map_grid = lambda in_array, row_axis: jnp.concatenate(
+        lax.all_to_all(jnp.stack([in_array] * lax.psum(1, row_axis)), row_axis, 0, 0), 1
+    )
     whole, whole_loc = (
-        lax.all_gather(wavefunction, "col", axis=1, tiled=True),
+        map_grid(wavefunction, "col"),
         lax.all_gather(right_loc, "col", axis=1, tiled=True),
     )
     local_tiles = wavefunction.shape[0]

time: 598 us -> 683 us (1.14)
  blocking collectives: 120 us -> 233 us
  waiting for transfers between devices: 271 us -> 222 us
  local copies, waits for them, and re-layouts: 125 us -> 137 us
  starting transfers between devices: 15.2 us -> 23 us
    all_gather x1, blocking collectives: 18.3 us -> 132 us  [per_device(): lax.all_gather(right_loc, 'col', axis=1, tiled=True)]
    all_gather x1 -> x0, waiting for transfers between devices: 46.7 us -> none  [per_device(): lax.all_gather(wavefunction, 'col', axis=1, tiled=True)]
    all_to_all x0 -> x1, starting transfers between devices: none -> 8.61 us  [per_device(): lax.all_to_all(jnp.stack([in_array] * lax.psum(1, row_axis)), row_axis, 0...]
    all_to_all x0 -> x1, local copies, waits for them, and re-layouts: none -> 7.61 us  [per_device(): lax.all_to_all(jnp.stack([in_array] * lax.psum(1, row_axis)), row_axis, 0...]
    unnamed x3 -> x2, waiting for transfers between devices: 139 us -> 137 us
  transfers between devices with their start and end apart: 4 -> 4, of which waited for: 3 -> 2; matrix products, arithmetic and copies ran while one was open for 22% -> 20% of each run, Pallas kernels for 0% -> 0%
where the time goes in v1:
time: 683 us; the launch traced here: 682 us
  blocking collectives  233 us (34%)
  waiting for transfers between devices  222 us (33%)
  local copies, waits for them, and re-layouts  137 us (20%)
  matrix products  34.7 us (5%)
  starting transfers between devices  23 us (3%)
  other arithmetic  17.3 us (3%)
  between operations  13.6 us (2%)
    unnamed x2, waiting for transfers between devices  137 us
    all_gather x1, blocking collectives, per_device(): lax.all_gather(right_loc, 'col', axis=1, tiled=True)  132 us
    all_to_all x1, blocking collectives, per_device(): lax.all_to_all(jnp.stack(pieces, axis=1), 'row', split_axis=0, concat_axi...  101 us
    all_to_all x1, waiting for transfers between devices, per_device(): lax.all_to_all(mixed, 'row', split_axis=1, concat_axis=0, tiled=True)  84.8 us
    gather x17, local copies, waits for them, and re-layouts, per_device(): blocks = whole[left_src[0, position]]  65.6 us
    dot_general x4, matrix products, per_device(): jnp.einsum('kxy,ksyz->sxz', env_left[0, position], blocks, preferred_elem...  18.8 us
    convert_element_type x4, local copies, waits for them, and re-layouts, per_device(): left_part = jnp.einsum('kxy,ksyz->sxz', env_left[0, position], blocks, pr...  14.6 us
  transfers between devices with their start and end apart: 4, of which 2 were waited for; matrix products, arithmetic and copies ran while one was open for 20% of the time, Pallas kernels for 0%

profile of v1, /device:TPU:1, one launch (start us, length us, event | category | flops | bytes accessed | tf_op | source)
XLA Modules:
  0.0 681.5 jit_solution(164634971758297709)
XLA Ops:
  6.5 5.4 stack.18
  11.9 8.6 %all-to-all-start.1 = ((bf16[16,4,1,256,256]{4,3,1,2,0:T(8,128)(2,1)}), bf16[16,4,1,256,256]{4,3,1,2,0:T(8,128)(2,1)}, u32[]{:S(2)}, u32[]{:S(2)}) async-start(bf16[16,4,1,256,256]{4,3,1,2,0:T(8,128)(2,1)} %stack.18), calls=%async_computation.1 | async-start | bytes 16777216 | tf_op jit(solution)/shard_map/all_to_all | solution.py:11
  20.5 131.8 %all-gather = s32[16,1,4]{2,1,0:T(1,128)S(1)} all-gather(s32[1,1,4]{2,1,0:T(1,128)S(1)} %bitcast.166), channel_id=1, replica_groups=mesh['row'=8,'col'=16] {'col'}, dimensions={0}, use_global_device_ids=true | all-gather | bytes 272 | tf_op jit(solution)/shard_map/all_gather | solution.py:15
  153.4 9.3 %all-to-all-start = ((s32[4,8,2]{0,2,1:T(2,128)}), s32[4,8,2]{0,2,1:T(2,128)S(1)}, u32[]{:S(2)}, u32[]{:S(2)}) async-start(s32[4,8,2]{0,2,1:T(2,128)} %bitcast.3), calls=%async_computation | async-start | bytes 16384 | tf_op jit(solution)/shard_map/all_to_all | solution.py:34
  162.7 7.6 %copy.76 = bf16[16,4,1,256,256]{4,3,0,1,2:T(8,128)(2,1)} copy(bf16[16,4,1,256,256]{4,3,1,2,0:T(8,128)(2,1)} %all-to-all-done.1) | data formatting | bytes 16777216 | tf_op jit(solution)/shard_map/all_to_all | solution.py:11
  170.3 6.0 fusion.62
  179.1 4.2 gather_fusion.5
  191.8 4.2 gather_fusion.6
  196.0 4.2 gather_fusion.7
  230.6 4.9 fusion.28
  235.4 4.6 copy.55
  250.5 4.9 fusion.34
  267.3 4.9 fusion.37
  277.7 5.7 pad_maximum_fusion
  283.4 9.6 %copy.65 = bf16[4,16,256,256]{3,2,0,1:T(8,128)(2,1)} copy(bf16[4,16,256,256]{3,1,2,0:T(8,128)(2,1)} %pad_maximum_fusion) | data formatting | bytes 16777216 | tf_op jit(solution)/shard_map/stack | solution.py:30
  293.0 5.0 all-to-all-start.2
  307.0 84.8 %all-to-all-done.2 = bf16[4,16,256,256]{3,2,0,1:T(8,128)(2,1)} async-done(((bf16[4,16,256,256]{3,2,0,1:T(8,128)(2,1)}), bf16[4,16,256,256]{3,2,0,1:T(8,128)(2,1)}, u32[]{:S(2)}, u32[]{:S(2)}) %all-to-all-start.2) | async-done | bytes 8388640 | tf_op jit(solution)/shard_map/all_to_all | solution.py:33
  391.8 7.8 %copy.66 = bf16[4,8,2,256,256]{4,3,0,1,2:T(8,128)(2,1)} copy(bf16[4,8,2,256,256]{4,3,0,2,1:T(8,128)(2,1)} %bitcast.48) | data formatting | bytes 16777216 | tf_op jit(solution)/shard_map/all_to_all | solution.py:33
  399.6 5.8 fusion
  410.2 6.2 pad_maximum_fusion.1
  416.4 7.6 %copy.67 = bf16[32,2,256,256]{3,2,1,0:T(8,128)(2,1)} copy(bf16[32,2,256,256]{3,2,0,1:T(8,128)(2,1)} %pad_maximum_fusion.1) | data formatting | bytes 16777216 | tf_op jit(solution)/shard_map/stack | solution.py:45
  424.0 101.5 %all_to_all.60 = bf16[32,2,256,256]{3,2,1,0:T(8,128)(2,1)} all-to-all(bf16[32,2,256,256]{3,2,1,0:T(8,128)(2,1)} %copy.67), channel_id=1, replica_groups=mesh['row'=8,'col'=16] {'row'}, dimensions={0} | all-to-all | bytes 16777216 | tf_op jit(solution)/shard_map/all_to_all | solution.py:45
  525.5 7.6 %copy.68 = bf16[4,8,2,256,256]{4,3,2,1,0:T(8,128)(2,1)} copy(bf16[4,8,2,256,256]{4,3,2,0,1:T(8,128)(2,1)} %bitcast.160) | data formatting | bytes 16777216 | tf_op jit(solution)/shard_map/all_to_all | solution.py:45
  534.4 137.5 %all-reduce.3.cloned.1.call-done = bf16[4,16,256,256]{3,2,1,0:T(8,128)(2,1)} async-done(((bf16[4,16,256,256]{3,2,1,0:T(8,128)(2,1)}), bf16[4,16,256,256]{3,2,1,0:T(8,128)(2,1)}) %all-reduce.3.cloned.1.call-update) | async-done | bytes 8388624
  (80 shorter events, 88.4 us)
Async XLA Ops:
  6.5 292.3 %copy-start = (bf16[1,4,256,256]{3,2,1,0:T(8,128)(2,1)S(1)}, bf16[1,4,256,256]{3,2,1,0:T(8,128)(2,1)}, u32[]{:S(2)}) copy-start(bf16[1,4,256,256]{3,2,1,0:T(8,128)(2,1)} %param.12) | copy-start | bytes 1572868
  11.9 8.6 %copy-start.15 = (s32[4,1]{0,1:T(1,128)S(1)}, s32[4,1]{0,1:T(1,128)}, u32[]{:S(2)}) copy-start(s32[4,1]{0,1:T(1,128)} %param.13) | copy-start | bytes 52
  11.9 141.2 %copy-start.12 = (s32[1,4,2]{1,2,0:T(2,128)S(1)}, s32[1,4,2]{1,2,0:T(2,128)}, u32[]{:S(2)}) copy-start(s32[1,4,2]{1,2,0:T(2,128)} %param.10) | copy-start | bytes 100
  11.9 141.5 %all-to-all-start.1 = ((bf16[16,4,1,256,256]{4,3,1,2,0:T(8,128)(2,1)}), bf16[16,4,1,256,256]{4,3,1,2,0:T(8,128)(2,1)}, u32[]{:S(2)}, u32[]{:S(2)}) async-start(bf16[16,4,1,256,256]{4,3,1,2,0:T(8,128)(2,1)} %stack.18), calls=%async_computation.1 | async-start | bytes 16777216 | tf_op jit(solution)/shard_map/all_to_all | solution.py:11
  153.4 139.6 %all-to-all-start = ((s32[4,8,2]{0,2,1:T(2,128)}), s32[4,8,2]{0,2,1:T(2,128)S(1)}, u32[]{:S(2)}, u32[]{:S(2)}) async-start(s32[4,8,2]{0,2,1:T(2,128)} %bitcast.3), calls=%async_computation | async-start | bytes 16384 | tf_op jit(solution)/shard_map/all_to_all | solution.py:34
  211.0 4.1 copy-start.10
  235.4 4.6 copy-start.11
  240.0 2.1 copy-start.1
  242.1 6.0 copy-start.4
  260.8 4.1 copy-start.3
  275.5 1.6 copy-start.5
  275.5 2.2 copy-start.6
  293.0 5.1 copy-start.13
  293.0 98.9 %all-to-all-start.2 = ((bf16[4,16,256,256]{3,2,0,1:T(8,128)(2,1)}), bf16[4,16,256,256]{3,2,0,1:T(8,128)(2,1)}, u32[]{:S(2)}, u32[]{:S(2)}) async-start(bf16[4,16,256,256]{3,2,0,1:T(8,128)(2,1)} %copy.65), calls=%async_computation.2 | async-start | bytes 16777216 | tf_op jit(solution)/shard_map/all_to_all | solution.py:33
  298.0 373.8 %all-reduce.3.cloned.1.call-start = ((), (), s32[]{:S(2)}) async-start(), calls=%async_computation.4 | async-start | bytes 16777216
  391.8 7.8 %copy-start.8 = (bf16[32,256,256]{2,1,0:T(8,128)(2,1)S(1)}, bf16[32,256,256]{2,1,0:T(8,128)(2,1)}, u32[]{:S(2)}) copy-start(bf16[32,256,256]{2,1,0:T(8,128)(2,1)} %gather_fusion) | copy-start | bytes 12582916
  399.6 5.8 copy-start.2
  399.6 7.3 %copy-start.7 = (bf16[32,256,256]{2,1,0:T(8,128)(2,1)S(1)}, bf16[32,256,256]{2,1,0:T(8,128)(2,1)}, u32[]{:S(2)}) copy-start(bf16[32,256,256]{2,1,0:T(8,128)(2,1)} %gather_fusion.1) | copy-start | bytes 12582916
  407.0 3.3 copy-start.9
  533.1 0.7 copy-start.16
  533.1 138.8 %copy-start.14 = (s32[4]{0:T(128)S(1)}, s32[4]{0:T(128)}, u32[]{:S(2)}) copy-start(s32[4]{0:T(128)} %param.14) | copy-start | bytes 52
Sparse Core Ops, SparseCore 0:
  533.3 138.5 all-reduce.2
